TPU v7x, 32 devices: a whole 2x2x4 slice. The times are simulated.
32 devices in a mesh: gx: 8 (over y, x, core), gy: 4 (over z).
Axes of the slice: x: 2, y: 2, z: 4, core: 2. Of those that a mesh axis runs over, the one named last changes fastest.
Arguments:
- tokens: bfloat16 [3072, 2048], P('gx', 'gy'), may hold values from -40 to 40
- gain: float32 [2048], replicated, may hold values from 0.1 to 1.9
- w_qkv: bfloat16 [2048, 3, 16, 128], P('gx', None, 'gy'), may hold values from -0.176776695 to 0.176776695
- w_out: bfloat16 [2048, 2048], P('gx', 'gy'), may hold values from -0.125 to 0.125
- lengths: int32 [6], replicated, may hold values from 1 to 2048, 3072 in all
Outputs:
- mixed: bfloat16 [3072, 2048], P('gx', 'gy')
- key_cache: bfloat16 [3072, 16, 128], P('gx', 'gy')
- value_cache: bfloat16 [3072, 16, 128], P('gx', 'gy')
Inputs may be any that keep to these rules, and one draw needn't show every extreme that they name: lengths are positive and sum to 3072; the longest is exactly 2048.
All inputs are finite; a program needn't handle non-finite values.
Results may differ from a plain program's by a relative error of at most 0.012.
The roundings to bfloat16 on the way count: a program that leaves them out, or rounds other values in their place, can miss the bound.
Values may be sent and summed in bfloat16 or wider, within the bound.
No kernel may reach another device: no remote copies, remote signals or barrier semaphores. Data moves between devices by JAX's collectives and lax.ppermute only.
A program may use at most 64 MiB of HBM per device.

v0:
```python
import math
import jax
import jax.numpy as jnp
from jax import lax
from jax.sharding import PartitionSpec as P


def rotate(vectors, position):
    half = vectors.shape[-1] // 2
    freq = 10000.0 ** (-(2.0 * jnp.arange(half, dtype=jnp.float32)) / vectors.shape[-1])
    angle = position.astype(jnp.float32)[:, None, None] * freq[None, None, :]
    cosine = jnp.cos(angle)
    sine = jnp.sin(angle)
    first = vectors[..., :half]
    second = vectors[..., half:]
    return jnp.concatenate(
        [first * cosine - second * sine, second * cosine + first * sine], axis=-1
    )


def block_rows(count):
    size = count
    while size > 1024 and size % 2 == 0:
        size = size // 2
    return size


def local(tokens, gain, w_qkv, w_out, lengths):
    tok_dev = tokens.shape[0]
    hloc = w_qkv.shape[2]
    hsize = w_qkv.shape[3]
    whole = lax.all_gather(tokens, "gy", axis=1, tiled=True)
    wide = whole.astype(jnp.float32)
    meansq = jnp.mean(wide * wide, axis=-1, keepdims=True)
    normed = (wide * lax.rsqrt(meansq + 1e-06) * gain[None, :]).astype(jnp.bfloat16)
    piece = lax.all_gather(w_qkv, "gx", axis=0, tiled=True)
    columns = normed
    projected = jnp.dot(
        columns, piece.reshape(piece.shape[0], -1), preferred_element_type=jnp.float32
    )
    projected = projected.reshape(tok_dev, 3, hloc, hsize)
    mine = lax.axis_index("gx")
    glob = mine * tok_dev + jnp.arange(tok_dev, dtype=jnp.int32)
    doc_start = jnp.cumsum(lengths) - lengths
    begin = jnp.max(jnp.where(doc_start[None, :] <= glob[:, None], doc_start[None, :], 0), axis=1)
    position = glob - begin
    query = rotate(projected[:, 0], position).astype(jnp.bfloat16)
    keys_own = rotate(projected[:, 1], position).astype(jnp.bfloat16)
    vals_own = projected[:, 2].astype(jnp.bfloat16)
    scale = 1.0 / math.sqrt(hsize)

    def tile_step(state, keys_blk, vals_blk, first):
        running, totals, accum = state
        kidx = first + jnp.arange(keys_blk.shape[0], dtype=jnp.int32)
        score = (
            jnp.einsum("qhd,khd->hqk", query, keys_blk, preferred_element_type=jnp.float32) * scale
        )
        keep = (kidx[None, :] >= begin[:, None]) & (kidx[None, :] <= glob[:, None])
        score = jnp.where(keep[None], score, -1e30)
        newmax = jnp.maximum(running, jnp.max(score, axis=-1))
        weight = jnp.where(keep[None], jnp.exp(score - newmax[..., None]), 0.0)
        factor = jnp.exp(running - newmax)
        totals = totals * factor + jnp.sum(weight, axis=-1)
        update = jnp.einsum(
            "hqk,khd->hqd",
            weight.astype(jnp.bfloat16),
            vals_blk,
            preferred_element_type=jnp.float32,
        )
        accum = accum * factor[..., None] + update
        return (newmax, totals, accum)

    initial = (
        jnp.full((hloc, tok_dev), -1e30, jnp.float32),
        jnp.zeros((hloc, tok_dev), jnp.float32),
        jnp.zeros((hloc, tok_dev, hsize), jnp.float32),
    )
    keys_piece = lax.all_gather(keys_own, "gx", axis=0, tiled=True)
    vals_piece = lax.all_gather(vals_own, "gx", axis=0, tiled=True)
    count = keys_piece.shape[0]
    size = block_rows(count)

    def one_tile(number, inner):
        first = (number * size).astype(jnp.int32)
        keys_blk = lax.dynamic_slice_in_dim(keys_piece, first, size, 0)
        vals_blk = lax.dynamic_slice_in_dim(vals_piece, first, size, 0)
        return tile_step(inner, keys_blk, vals_blk, first)

    running, totals, accum = lax.fori_loop(0, count // size, one_tile, initial)
    attended = (accum / totals[..., None]).astype(jnp.bfloat16)
    attended = jnp.transpose(attended, (1, 0, 2)).reshape(tok_dev, hloc * hsize)
    all_heads = lax.all_gather(attended, "gy", axis=1, tiled=True)
    columns = all_heads
    mixed = jnp.dot(
        columns, lax.all_gather(w_out, "gx", axis=0, tiled=True), preferred_element_type=jnp.float32
    ).astype(jnp.bfloat16)
    return (mixed, keys_own, vals_own)


def solution(mesh):
    return jax.shard_map(
        local,
        mesh=mesh,
        in_specs=(P("gx", "gy"), P(), P("gx", None, "gy", None), P("gx", "gy"), P()),
        out_specs=(P("gx", "gy"), P("gx", "gy", None), P("gx", "gy", None)),
        check_vma=False,
    )
```

profile of v0, /device:TPU:0, one launch (start us, length us, event | category | flops | bytes accessed | tf_op | source)
XLA Modules:
  0.0 282.4 jit_solution(10697021689812042305)
XLA Ops:
  7.2 0.7 all-gather.8.cloned.1.call-update
  7.9 0.7 all-gather.10.cloned.1.call-update
  8.7 0.8 reduce-window.9
  9.5 0.7 bitcast_subtract_fusion
  10.7 38.7 %all-gather.8.cloned.1.call-done = bf16[384,2048]{1,0:T(8,128)(2,1)} async-done(((bf16[384,512]{1,0:T(8,128)(2,1)}), bf16[384,2048]{1,0:T(8,128)(2,1)}) %all-gather.8.cloned.1.call-update) | async-done | bytes 1572880 | tf_op jit(solution)/shard_map/all_gather | solution.py:32
  49.4 1.8 fusion.22
  51.2 44.5 %all-gather.10.cloned.1.call-done = bf16[2048,3,4,128]{3,2,1,0:T(4,128)(2,1)} async-done(((bf16[256,3,4,128]{3,2,1,0:T(4,128)(2,1)}), bf16[2048,3,4,128]{3,2,1,0:T(4,128)(2,1)}) %all-gather.10.cloned.1.call-update) | async-done | bytes 6291472 | tf_op jit(solution)/shard_map/all_gather | solution.py:36
  95.7 10.6 %copy.41 = bf16[2048,3,4,128]{0,3,2,1:T(8,128)(2,1)} copy(bf16[2048,3,4,128]{3,2,1,0:T(4,128)(2,1)} %all-gather.10.cloned.1.call-done) | data formatting | bytes 12582912 | tf_op jit(solution)/shard_map/reshape | solution.py:39
  106.3 6.2 %fusion.20 = f32[384,3,4,128]{0,3,2,1:T(8,128)S(1)} fusion(bf16[2048,3,4,128]{0,3,2,1:T(8,128)(2,1)} %copy.41, bf16[384,2048]{1,0:T(8,128)(2,1)} %all-gather.8.cloned.1.call-done, f32[2048]{0:T(1024)S(1)} %copy-done.2, f32[384]{0:T(512)S(1)} %add_rsqrt_fusion), kind=kOutput, calls=%fused_computation.25 | convolution fusion | flops 2419064832 | bytes 10233344 | tf_op jit(solution)/shard_map/dot_general | solution.py:38
  112.8 0.8 pad_maximum_fusion
  113.7 0.8 slice.47
  115.5 31.2 %all-gather.12.cloned.1.call-done = bf16[3072,4,128]{0,2,1:T(8,128)(2,1)} async-done(((bf16[384,4,128]{0,2,1:T(8,128)(2,1)}), bf16[3072,4,128]{0,2,1:T(8,128)(2,1)}) %all-gather.12.cloned.1.call-update) | async-done | bytes 3145744 | tf_op jit(solution)/shard_map/all_gather | solution.py:78
  146.6 35.1 %all-gather.18.cloned.1.call-done = bf16[3072,1,4,128]{0,3,2,1:T(8,128)(2,1)} async-done(((bf16[384,1,4,128]{0,3,2,1:T(8,128)(2,1)}), bf16[3072,1,4,128]{0,3,2,1:T(8,128)(2,1)}) %all-gather.18.cloned.1.call-update) | async-done | bytes 3145744 | tf_op jit(solution)/shard_map/all_gather | solution.py:79
  181.8 50.4 %while.18 = (s32[]{:T(128)}, f32[4,384]{1,0:T(4,128)S(1)}, f32[4,384]{1,0:T(4,128)S(1)}, f32[4,384,128]{2,1,0:T(8,128)}, s32[384]{0:T(512)S(1)}, /*index=5*/bf16...) while((s32[]{:T(128)}, f32[4,384]{1,0:T(4,128)S(1)}, ...), condition=%wide.region_6.7_spmd.clone, body=%wide.region_3.6_spmd.clone.sunk | while | flops 620798592 | bytes 37858016 | solution.py:89
  182.1 4.4 %fusion.42 = (f32[4,384]{1,0:T(4,128)S(1)}, f32[4,768,384]{2,1,0:T(8,128)}) fusion(pred[384,768]{0,1:T(8,128)(4,1)S(1)} %compare_and_fusion.2, bf16[384,4,128]{2,0,1:T(8,128)(2,1)S(1)} %get-tuple-element.368, bf16[3072,4,128]{0,2,1:T(8,128)(2,1)} %get-tuple-element.367, s32[]{:T(128)S(6)} %select_n.63), kind=kOutput, calls=%fused_computation.3.clone.1 | convolution fusion | flops 305527296 | bytes 6199300 | tf_op jit(solution)/shard_map/while/body/eval_jaxpr/qhd,khd->hqk/dot_general | solution.py:56
  186.5 3.7 %fusion.43 = f32[4,384]{1,0:T(4,128)S(1)} fusion(f32[4,768,384]{2,1,0:T(8,128)} %get-tuple-element.333, f32[4,384]{1,0:T(4,128)S(1)} %select_maximum_fusion.2, pred[384,768]{0,1:T(8,128)(4,1)S(1)} %compare_and_fusion.2), kind=kLoop, calls=%fused_computation.5.clone.1 | loop fusion | flops 5896704 | bytes 5025792 | tf_op jit(solution)/shard_map/while/body/eval_jaxpr/reduce_sum | solution.py:63
  190.3 3.9 %fusion.45 = f32[4,384,128]{2,1,0:T(8,128)} fusion(f32[4,768,384]{2,1,0:T(8,128)S(1)} %copy-done, f32[4,384]{1,0:T(4,128)S(1)} %select_maximum_fusion.2, pred[384,768]{0,1:T(8,128)(4,1)S(1)} %compare_and_fusion.2, f32[4,384,128]{2,1,0:T(8,128)} %get-tuple-element.352, bf16[3072,4,128]{0,2,1:T(8,128)(2,1)} %get-tuple-element.369, s32[]{:T(128)S(6)} %select_n.63, ...), kind=kOutput, calls=%fused_computation.8.clone.1 | convolution fusion | flops 308477952 | bytes 7385093 | tf_op jit(solution)/shard_map/while/body/eval_jaxpr/hqk,khd->hqd/dot_general | solution.py:64
  194.5 4.4 %fusion.42 = (f32[4,384]{1,0:T(4,128)S(1)}, f32[4,768,384]{2,1,0:T(8,128)}) fusion(pred[384,768]{0,1:T(8,128)(4,1)S(1)} %compare_and_fusion.2, bf16[384,4,128]{2,0,1:T(8,128)(2,1)S(1)} %get-tuple-element.368, bf16[3072,4,128]{0,2,1:T(8,128)(2,1)} %get-tuple-element.367, s32[]{:T(128)S(6)} %select_n.63), kind=kOutput, calls=%fused_computation.3.clone.1 | convolution fusion | flops 305527296 | bytes 6199300 | tf_op jit(solution)/shard_map/while/body/eval_jaxpr/qhd,khd->hqk/dot_general | solution.py:56
  198.9 3.7 %fusion.43 = f32[4,384]{1,0:T(4,128)S(1)} fusion(f32[4,768,384]{2,1,0:T(8,128)} %get-tuple-element.333, f32[4,384]{1,0:T(4,128)S(1)} %select_maximum_fusion.2, pred[384,768]{0,1:T(8,128)(4,1)S(1)} %compare_and_fusion.2), kind=kLoop, calls=%fused_computation.5.clone.1 | loop fusion | flops 5896704 | bytes 5025792 | tf_op jit(solution)/shard_map/while/body/eval_jaxpr/reduce_sum | solution.py:63
  203.0 4.1 %fusion.45 = f32[4,384,128]{2,1,0:T(8,128)} fusion(f32[4,768,384]{2,1,0:T(8,128)S(1)} %copy-done, f32[4,384]{1,0:T(4,128)S(1)} %select_maximum_fusion.2, pred[384,768]{0,1:T(8,128)(4,1)S(1)} %compare_and_fusion.2, f32[4,384,128]{2,1,0:T(8,128)} %get-tuple-element.352, bf16[3072,4,128]{0,2,1:T(8,128)(2,1)} %get-tuple-element.369, s32[]{:T(128)S(6)} %select_n.63, ...), kind=kOutput, calls=%fused_computation.8.clone.1 | convolution fusion | flops 308477952 | bytes 7385093 | tf_op jit(solution)/shard_map/while/body/eval_jaxpr/hqk,khd->hqd/dot_general | solution.py:64
  207.4 4.4 %fusion.42 = (f32[4,384]{1,0:T(4,128)S(1)}, f32[4,768,384]{2,1,0:T(8,128)}) fusion(pred[384,768]{0,1:T(8,128)(4,1)S(1)} %compare_and_fusion.2, bf16[384,4,128]{2,0,1:T(8,128)(2,1)S(1)} %get-tuple-element.368, bf16[3072,4,128]{0,2,1:T(8,128)(2,1)} %get-tuple-element.367, s32[]{:T(128)S(6)} %select_n.63), kind=kOutput, calls=%fused_computation.3.clone.1 | convolution fusion | flops 305527296 | bytes 6199300 | tf_op jit(solution)/shard_map/while/body/eval_jaxpr/qhd,khd->hqk/dot_general | solution.py:56
  211.8 3.7 %fusion.43 = f32[4,384]{1,0:T(4,128)S(1)} fusion(f32[4,768,384]{2,1,0:T(8,128)} %get-tuple-element.333, f32[4,384]{1,0:T(4,128)S(1)} %select_maximum_fusion.2, pred[384,768]{0,1:T(8,128)(4,1)S(1)} %compare_and_fusion.2), kind=kLoop, calls=%fused_computation.5.clone.1 | loop fusion | flops 5896704 | bytes 5025792 | tf_op jit(solution)/shard_map/while/body/eval_jaxpr/reduce_sum | solution.py:63
  215.6 4.1 %fusion.45 = f32[4,384,128]{2,1,0:T(8,128)} fusion(f32[4,768,384]{2,1,0:T(8,128)S(1)} %copy-done, f32[4,384]{1,0:T(4,128)S(1)} %select_maximum_fusion.2, pred[384,768]{0,1:T(8,128)(4,1)S(1)} %compare_and_fusion.2, f32[4,384,128]{2,1,0:T(8,128)} %get-tuple-element.352, bf16[3072,4,128]{0,2,1:T(8,128)(2,1)} %get-tuple-element.369, s32[]{:T(128)S(6)} %select_n.63, ...), kind=kOutput, calls=%fused_computation.8.clone.1 | convolution fusion | flops 308477952 | bytes 7385093 | tf_op jit(solution)/shard_map/while/body/eval_jaxpr/hqk,khd->hqd/dot_general | solution.py:64
  220.0 4.4 %fusion.42 = (f32[4,384]{1,0:T(4,128)S(1)}, f32[4,768,384]{2,1,0:T(8,128)}) fusion(pred[384,768]{0,1:T(8,128)(4,1)S(1)} %compare_and_fusion.2, bf16[384,4,128]{2,0,1:T(8,128)(2,1)S(1)} %get-tuple-element.368, bf16[3072,4,128]{0,2,1:T(8,128)(2,1)} %get-tuple-element.367, s32[]{:T(128)S(6)} %select_n.63), kind=kOutput, calls=%fused_computation.3.clone.1 | convolution fusion | flops 305527296 | bytes 6199300 | tf_op jit(solution)/shard_map/while/body/eval_jaxpr/qhd,khd->hqk/dot_general | solution.py:56
  224.4 3.7 %fusion.43 = f32[4,384]{1,0:T(4,128)S(1)} fusion(f32[4,768,384]{2,1,0:T(8,128)} %get-tuple-element.333, f32[4,384]{1,0:T(4,128)S(1)} %select_maximum_fusion.2, pred[384,768]{0,1:T(8,128)(4,1)S(1)} %compare_and_fusion.2), kind=kLoop, calls=%fused_computation.5.clone.1 | loop fusion | flops 5896704 | bytes 5025792 | tf_op jit(solution)/shard_map/while/body/eval_jaxpr/reduce_sum | solution.py:63
  228.1 4.1 %fusion.45 = f32[4,384,128]{2,1,0:T(8,128)} fusion(f32[4,768,384]{2,1,0:T(8,128)S(1)} %copy-done, f32[4,384]{1,0:T(4,128)S(1)} %select_maximum_fusion.2, pred[384,768]{0,1:T(8,128)(4,1)S(1)} %compare_and_fusion.2, f32[4,384,128]{2,1,0:T(8,128)} %get-tuple-element.352, bf16[3072,4,128]{0,2,1:T(8,128)(2,1)} %get-tuple-element.369, s32[]{:T(128)S(6)} %select_n.63, ...), kind=kOutput, calls=%fused_computation.8.clone.1 | convolution fusion | flops 308477952 | bytes 7385093 | tf_op jit(solution)/shard_map/while/body/eval_jaxpr/hqk,khd->hqd/dot_general | solution.py:64
  232.2 1.4 copy.36
  233.7 0.8 divide_convert_fusion
  234.5 1.0 copy.37
  235.5 1.0 copy.38
  236.5 35.2 %all-gather.14.cloned.1.call-done = bf16[384,2048]{0,1:T(8,128)(2,1)} async-done(((bf16[384,512]{0,1:T(8,128)(2,1)}), bf16[384,2048]{0,1:T(8,128)(2,1)}) %all-gather.14.cloned.1.call-update) | async-done | bytes 1572880 | tf_op jit(solution)/shard_map/all_gather | solution.py:92
  271.7 3.8 %convolution_convert_fusion = bf16[384,512]{1,0:T(8,128)(2,1)} fusion(bf16[384,2048]{0,1:T(8,128)(2,1)} %all-gather.14.cloned.1.call-done, bf16[2048,512]{1,0:T(8,128)(2,1)} %all-gather.16.cloned.1.call-done), kind=kOutput, calls=%fused_computation.35 | convolution fusion | flops 805502976 | bytes 4063232 | tf_op jit(solution)/shard_map/dot_general | solution.py:94
  (61 shorter events, 4.0 us)
Async XLA Ops:
  7.2 42.2 %all-gather.8.cloned.1.call-start = ((), (), s32[]{:S(2)}) async-start(), calls=%async_computation | async-start | bytes 1966080 | tf_op jit(solution)/shard_map/all_gather | solution.py:32
  7.9 87.8 %all-gather.10.cloned.1.call-start = ((), (), s32[]{:S(2)}) async-start(), calls=%async_computation.1 | async-start | bytes 7077888 | tf_op jit(solution)/shard_map/all_gather | solution.py:36
  8.6 138.0 %all-gather.12.cloned.1.call-start = ((), (), s32[]{:S(2)}) async-start(), calls=%async_computation.2 | async-start | bytes 3538944 | tf_op jit(solution)/shard_map/all_gather | solution.py:78
  51.2 55.1 %copy-start.2 = (f32[2048]{0:T(1024)S(1)}, f32[2048]{0:T(1024)}, u32[]{:S(2)}) copy-start(f32[2048]{0:T(1024)} %param.8) | copy-start | bytes 24580
  113.6 68.1 %all-gather.18.cloned.1.call-start = ((), (), s32[]{:S(2)}) async-start(), calls=%async_computation.5 | async-start | bytes 3538944 | tf_op jit(solution)/shard_map/all_gather | solution.py:79
  114.5 122.0 %all-gather.16.cloned.1.call-start = ((), (), s32[]{:S(2)}) async-start(), calls=%async_computation.4 | async-start | bytes 2359296 | tf_op jit(solution)/shard_map/all_gather | solution.py:95
  115.1 156.6 %all-gather.14.cloned.1.call-start = ((), (), s32[]{:S(2)}) async-start(), calls=%async_computation.3 | async-start | bytes 1966080 | tf_op jit(solution)/shard_map/all_gather | solution.py:92
  186.5 3.8 %copy-start = (f32[4,768,384]{2,1,0:T(8,128)S(1)}, f32[4,768,384]{2,1,0:T(8,128)}, u32[]{:S(2)}) copy-start(f32[4,768,384]{2,1,0:T(8,128)} %get-tuple-element.333) | copy-start | bytes 14155780 | tf_op jit(solution)/shard_map/while
  198.9 4.1 %copy-start = (f32[4,768,384]{2,1,0:T(8,128)S(1)}, f32[4,768,384]{2,1,0:T(8,128)}, u32[]{:S(2)}) copy-start(f32[4,768,384]{2,1,0:T(8,128)} %get-tuple-element.333) | copy-start | bytes 14155780 | tf_op jit(solution)/shard_map/while
  211.8 3.8 %copy-start = (f32[4,768,384]{2,1,0:T(8,128)S(1)}, f32[4,768,384]{2,1,0:T(8,128)}, u32[]{:S(2)}) copy-start(f32[4,768,384]{2,1,0:T(8,128)} %get-tuple-element.333) | copy-start | bytes 14155780 | tf_op jit(solution)/shard_map/while
  224.4 3.8 %copy-start = (f32[4,768,384]{2,1,0:T(8,128)S(1)}, f32[4,768,384]{2,1,0:T(8,128)}, u32[]{:S(2)}) copy-start(f32[4,768,384]{2,1,0:T(8,128)} %get-tuple-element.333) | copy-start | bytes 14155780 | tf_op jit(solution)/shard_map/while
  232.2 2.3 copy-start.1
Sparse Core Ops, SparseCore 0:
  9.6 39.7 all-gather.7
  51.3 44.3 all-gather.9
  113.8 32.8 all-gather.11
  148.9 32.8 all-gather.17
  183.5 27.8 all-gather.15
  234.6 37.0 all-gather.13
where the time goes:
time: 283 us; the launch traced here: 282 us
  waiting for transfers between devices  187 us (66%)
  matrix products  43.8 us (15%)
  other arithmetic  21.6 us (8%)
  local copies, waits for them, and re-layouts  15.8 us (6%)
  between operations  14.2 us (5%)
    all_gather x1, waiting for transfers between devices, local(): piece = lax.all_gather(w_qkv, 'gx', axis=0, tiled=True)  44.5 us
    all_gather x1, waiting for transfers between devices, local(): whole = lax.all_gather(tokens, 'gy', axis=1, tiled=True)  38.7 us
    all_gather x1, waiting for transfers between devices, local(): all_heads = lax.all_gather(attended, 'gy', axis=1, tiled=True)  35.2 us
    all_gather x1, waiting for transfers between devices, local(): vals_piece = lax.all_gather(vals_own, 'gx', axis=0, tiled=True)  35.1 us
    all_gather x1, waiting for transfers between devices, local(): keys_piece = lax.all_gather(keys_own, 'gx', axis=0, tiled=True)  31.2 us
    dot_general x4, matrix products, tile_step(): jnp.einsum('qhd,khd->hqk', query, keys_blk, preferred_element_type=jnp.fl...  17.7 us
    dot_general x4, matrix products, tile_step(): jnp.einsum('hqk,khd->hqd', weight.astype(jnp.bfloat16), vals_blk, preferr...  16.1 us
    reduce_sum x4, other arithmetic, tile_step(): totals = totals * factor + jnp.sum(weight, axis=-1)  14.6 us
  transfers between devices with their start and end apart: 6, of which 5 were waited for; matrix products, arithmetic and copies ran while one was open for 21% of the time, Pallas kernels for 0%

commit v1 on v0

--- a/solution.py
+++ b/solution.py
@@ -29,7 +29,12 @@
     tok_dev = tokens.shape[0]
     hloc = w_qkv.shape[2]
     hsize = w_qkv.shape[3]
-    whole = lax.all_gather(tokens, "gy", axis=1, tiled=True)
+    ring = [tokens]
+    for hop in range(3):
+        ring.append(lax.ppermute(ring[-1], "gy", [(dev, (dev + 1) % 4) for dev in range(4)]))
+    whole = jnp.roll(
+        jnp.concatenate(ring[::-1], axis=1), (lax.axis_index("gy") + 1) * ring[0].shape[1], axis=1
+    )
     wide = whole.astype(jnp.float32)
     meansq = jnp.mean(wide * wide, axis=-1, keepdims=True)
     normed = (wide * lax.rsqrt(meansq + 1e-06) * gain[None, :]).astype(jnp.bfloat16)

time: 283 us -> 246 us (0.87)
  waiting for transfers between devices: 187 us -> 145 us
  starting transfers between devices: 0.24 us -> 3.28 us
    all_gather x1 -> x0, waiting for transfers between devices: 38.7 us -> none  [local(): whole = lax.all_gather(tokens, 'gy', axis=1, tiled=True)]
    all_gather x1, waiting for transfers between devices: 44.5 us -> 10.1 us  [local(): piece = lax.all_gather(w_qkv, 'gx', axis=0, tiled=True)]
    ppermute x0 -> x3, waiting for transfers between devices: none -> 31.9 us  [local(): lax.ppermute(ring[-1], 'gy', [(dev, (dev + 1) % 4) for dev in range(4)])]
    ppermute x0 -> x3, starting transfers between devices: none -> 3.08 us  [local(): lax.ppermute(ring[-1], 'gy', [(dev, (dev + 1) % 4) for dev in range(4)])]
  transfers between devices with their start and end apart: 6 -> 8, of which waited for: 5 -> 7; matrix products, arithmetic and copies ran while one was open for 21% -> 24% of each run, Pallas kernels for 0% -> 0%
where the time goes in v1:
time: 246 us; the launch traced here: 245 us
  waiting for transfers between devices  145 us (59%)
  matrix products  43.7 us (18%)
  other arithmetic  20.9 us (8%)
  local copies, waits for them, and re-layouts  18.6 us (8%)
  between operations  14 us (6%)
  starting transfers between devices  3.28 us (1%)
    all_gather x1, waiting for transfers between devices, local(): vals_piece = lax.all_gather(vals_own, 'gx', axis=0, tiled=True)  35.3 us
    all_gather x1, waiting for transfers between devices, local(): all_heads = lax.all_gather(attended, 'gy', axis=1, tiled=True)  35.2 us
    ppermute x3, waiting for transfers between devices, local(): lax.ppermute(ring[-1], 'gy', [(dev, (dev + 1) % 4) for dev in range(4)])  31.9 us
    all_gather x1, waiting for transfers between devices, local(): keys_piece = lax.all_gather(keys_own, 'gx', axis=0, tiled=True)  31.2 us
    dot_general x4, matrix products, tile_step(): jnp.einsum('qhd,khd->hqk', query, keys_blk, preferred_element_type=jnp.fl...  17.7 us
    dot_general x4, matrix products, tile_step(): jnp.einsum('hqk,khd->hqd', weight.astype(jnp.bfloat16), vals_blk, preferr...  16 us
    reduce_sum x4, other arithmetic, tile_step(): totals = totals * factor + jnp.sum(weight, axis=-1)  14.6 us
    reshape x1, local copies, waits for them, and re-layouts, local(): piece.reshape(piece.shape[0], -1)  10.6 us
  transfers between devices with their start and end apart: 8, of which 7 were waited for; matrix products, arithmetic and copies ran while one was open for 24% of the time, Pallas kernels for 0%

profile of v1, /device:TPU:0, one launch (start us, length us, event | category | flops | bytes accessed | tf_op | source)
XLA Modules:
  0.0 245.4 jit_solution(17997485241025590271)
XLA Ops:
  8.0 3.1 %collective-permute-start = (bf16[384,512]{1,0:T(8,128)(2,1)}, bf16[384,512]{1,0:T(8,128)(2,1)S(1)}, u32[]{:S(2)}, u32[]{:S(2)}) collective-permute-start(bf16[384,512]{1,0:T(8,128)(2,1)} %param.7), channel_id=1, source_target_pairs={{0,1},{1,2},{2,3},{3,0},{4,5},{5,6},{6,7},{7,4},{8,9},{9,10},{10,1... | collective-permute-start | bytes 1179656 | tf_op jit(solution)/shard_map/ppermute | solution.py:34
  11.0 11.3 %collective-permute-done = bf16[384,512]{1,0:T(8,128)(2,1)S(1)} collective-permute-done((bf16[384,512]{1,0:T(8,128)(2,1)}, bf16[384,512]{1,0:T(8,128)(2,1)S(1)}, u32[]{:S(2)}, u32[]{:S(2)}) %collective-permute-start) | collective-permute-done | bytes 393248 | tf_op jit(solution)/shard_map/ppermute | solution.py:34
  22.4 0.8 reduce-window.9
  24.0 10.5 %collective-permute-done.1 = bf16[384,512]{1,0:T(8,128)(2,1)S(1)} collective-permute-done((bf16[384,512]{1,0:T(8,128)(2,1)S(1)}, bf16[384,512]{1,0:T(8,128)(2,1)S(1)}, u32[]{:S(2)}, u32[]{:S(2)}) %collective-permute-start.1) | collective-permute-done | bytes 393248 | tf_op jit(solution)/shard_map/ppermute | solution.py:34
  34.5 1.1 multiply_cosine_fusion
  35.6 10.1 %collective-permute-done.2 = bf16[384,512]{1,0:T(8,128)(2,1)S(1)} collective-permute-done((bf16[384,512]{1,0:T(8,128)(2,1)S(1)}, bf16[384,512]{1,0:T(8,128)(2,1)S(1)}, u32[]{:S(2)}, u32[]{:S(2)}) %collective-permute-start.2) | collective-permute-done | bytes 393248 | tf_op jit(solution)/shard_map/ppermute | solution.py:34
  46.1 1.6 copy-done.3
  48.1 10.1 %all-gather.7.cloned.1.call-done = bf16[2048,3,4,128]{3,2,1,0:T(4,128)(2,1)} async-done(((bf16[256,3,4,128]{3,2,1,0:T(4,128)(2,1)}), bf16[2048,3,4,128]{3,2,1,0:T(4,128)(2,1)}) %all-gather.7.cloned.1.call-update) | async-done | bytes 6291472 | tf_op jit(solution)/shard_map/all_gather | solution.py:41
  58.1 10.6 %copy.41 = bf16[2048,3,4,128]{0,3,2,1:T(8,128)(2,1)} copy(bf16[2048,3,4,128]{3,2,1,0:T(4,128)(2,1)} %all-gather.7.cloned.1.call-done) | data formatting | bytes 12582912 | tf_op jit(solution)/shard_map/reshape | solution.py:44
  68.8 6.2 %fusion.20 = f32[384,3,4,128]{0,3,2,1:T(8,128)S(1)} fusion(bf16[2048,3,4,128]{0,3,2,1:T(8,128)(2,1)} %copy.41, f32[2048]{0:T(1024)S(1)} %copy-done.6, f32[384]{0:T(512)S(1)} %add_rsqrt_fusion, bf16[384,4096]{1,0:T(8,128)(2,1)} %copy-done.3, s32[]{:T(128)S(6)} %select_n.42), kind=kOutput, calls=%fused_computation.25 | convolution fusion | flops 2419064832 | bytes 10233348 | tf_op jit(solution)/shard_map/dot_general | solution.py:43
  77.0 0.8 slice.47
  78.7 31.2 %all-gather.9.cloned.1.call-done = bf16[3072,4,128]{0,2,1:T(8,128)(2,1)} async-done(((bf16[384,4,128]{0,2,1:T(8,128)(2,1)}), bf16[3072,4,128]{0,2,1:T(8,128)(2,1)}) %all-gather.9.cloned.1.call-update) | async-done | bytes 3145744 | tf_op jit(solution)/shard_map/all_gather | solution.py:83
  109.9 35.3 %all-gather.15.cloned.1.call-done = bf16[3072,1,4,128]{0,3,2,1:T(8,128)(2,1)} async-done(((bf16[384,1,4,128]{0,3,2,1:T(8,128)(2,1)}), bf16[3072,1,4,128]{0,3,2,1:T(8,128)(2,1)}) %all-gather.15.cloned.1.call-update) | async-done | bytes 3145744 | tf_op jit(solution)/shard_map/all_gather | solution.py:84
  145.2 50.3 %while.18 = (s32[]{:T(128)}, f32[4,384]{1,0:T(4,128)S(1)}, f32[4,384]{1,0:T(4,128)S(1)}, f32[4,384,128]{2,1,0:T(8,128)}, s32[384]{0:T(512)S(1)}, /*index=5*/bf16...) while((s32[]{:T(128)}, f32[4,384]{1,0:T(4,128)S(1)}, ...), condition=%wide.region_6.7_spmd.clone, body=%wide.region_3.6_spmd.clone.sunk | while | flops 620798592 | bytes 37858016 | solution.py:94
  145.5 4.4 %fusion.44 = (f32[4,384]{1,0:T(4,128)S(1)}, f32[4,768,384]{2,1,0:T(8,128)}) fusion(pred[384,768]{0,1:T(8,128)(4,1)S(1)} %compare_and_fusion.2, bf16[384,4,128]{2,0,1:T(8,128)(2,1)S(1)} %get-tuple-element.368, bf16[3072,4,128]{0,2,1:T(8,128)(2,1)} %get-tuple-element.367, s32[]{:T(128)S(6)} %select_n.78), kind=kOutput, calls=%fused_computation.3.clone.1 | convolution fusion | flops 305527296 | bytes 6199300 | tf_op jit(solution)/shard_map/while/body/eval_jaxpr/qhd,khd->hqk/dot_general | solution.py:61
  149.9 3.7 %fusion.45 = f32[4,384]{1,0:T(4,128)S(1)} fusion(f32[4,768,384]{2,1,0:T(8,128)} %get-tuple-element.333, f32[4,384]{1,0:T(4,128)S(1)} %select_maximum_fusion.2, pred[384,768]{0,1:T(8,128)(4,1)S(1)} %compare_and_fusion.2), kind=kLoop, calls=%fused_computation.5.clone.1 | loop fusion | flops 5896704 | bytes 5025792 | tf_op jit(solution)/shard_map/while/body/eval_jaxpr/reduce_sum | solution.py:68
  153.7 3.8 %fusion.47 = f32[4,384,128]{2,1,0:T(8,128)} fusion(f32[4,768,384]{2,1,0:T(8,128)S(1)} %copy-done, f32[4,384]{1,0:T(4,128)S(1)} %select_maximum_fusion.2, pred[384,768]{0,1:T(8,128)(4,1)S(1)} %compare_and_fusion.2, f32[4,384,128]{2,1,0:T(8,128)} %get-tuple-element.352, bf16[3072,4,128]{0,2,1:T(8,128)(2,1)} %get-tuple-element.369, s32[]{:T(128)S(6)} %select_n.78, ...), kind=kOutput, calls=%fused_computation.8.clone.1 | convolution fusion | flops 308477952 | bytes 7385093 | tf_op jit(solution)/shard_map/while/body/eval_jaxpr/hqk,khd->hqd/dot_general | solution.py:69
  157.9 4.4 %fusion.44 = (f32[4,384]{1,0:T(4,128)S(1)}, f32[4,768,384]{2,1,0:T(8,128)}) fusion(pred[384,768]{0,1:T(8,128)(4,1)S(1)} %compare_and_fusion.2, bf16[384,4,128]{2,0,1:T(8,128)(2,1)S(1)} %get-tuple-element.368, bf16[3072,4,128]{0,2,1:T(8,128)(2,1)} %get-tuple-element.367, s32[]{:T(128)S(6)} %select_n.78), kind=kOutput, calls=%fused_computation.3.clone.1 | convolution fusion | flops 305527296 | bytes 6199300 | tf_op jit(solution)/shard_map/while/body/eval_jaxpr/qhd,khd->hqk/dot_general | solution.py:61
  162.3 3.7 %fusion.45 = f32[4,384]{1,0:T(4,128)S(1)} fusion(f32[4,768,384]{2,1,0:T(8,128)} %get-tuple-element.333, f32[4,384]{1,0:T(4,128)S(1)} %select_maximum_fusion.2, pred[384,768]{0,1:T(8,128)(4,1)S(1)} %compare_and_fusion.2), kind=kLoop, calls=%fused_computation.5.clone.1 | loop fusion | flops 5896704 | bytes 5025792 | tf_op jit(solution)/shard_map/while/body/eval_jaxpr/reduce_sum | solution.py:68
  166.4 4.1 %fusion.47 = f32[4,384,128]{2,1,0:T(8,128)} fusion(f32[4,768,384]{2,1,0:T(8,128)S(1)} %copy-done, f32[4,384]{1,0:T(4,128)S(1)} %select_maximum_fusion.2, pred[384,768]{0,1:T(8,128)(4,1)S(1)} %compare_and_fusion.2, f32[4,384,128]{2,1,0:T(8,128)} %get-tuple-element.352, bf16[3072,4,128]{0,2,1:T(8,128)(2,1)} %get-tuple-element.369, s32[]{:T(128)S(6)} %select_n.78, ...), kind=kOutput, calls=%fused_computation.8.clone.1 | convolution fusion | flops 308477952 | bytes 7385093 | tf_op jit(solution)/shard_map/while/body/eval_jaxpr/hqk,khd->hqd/dot_general | solution.py:69
  170.8 4.4 %fusion.44 = (f32[4,384]{1,0:T(4,128)S(1)}, f32[4,768,384]{2,1,0:T(8,128)}) fusion(pred[384,768]{0,1:T(8,128)(4,1)S(1)} %compare_and_fusion.2, bf16[384,4,128]{2,0,1:T(8,128)(2,1)S(1)} %get-tuple-element.368, bf16[3072,4,128]{0,2,1:T(8,128)(2,1)} %get-tuple-element.367, s32[]{:T(128)S(6)} %select_n.78), kind=kOutput, calls=%fused_computation.3.clone.1 | convolution fusion | flops 305527296 | bytes 6199300 | tf_op jit(solution)/shard_map/while/body/eval_jaxpr/qhd,khd->hqk/dot_general | solution.py:61
  175.2 3.7 %fusion.45 = f32[4,384]{1,0:T(4,128)S(1)} fusion(f32[4,768,384]{2,1,0:T(8,128)} %get-tuple-element.333, f32[4,384]{1,0:T(4,128)S(1)} %select_maximum_fusion.2, pred[384,768]{0,1:T(8,128)(4,1)S(1)} %compare_and_fusion.2), kind=kLoop, calls=%fused_computation.5.clone.1 | loop fusion | flops 5896704 | bytes 5025792 | tf_op jit(solution)/shard_map/while/body/eval_jaxpr/reduce_sum | solution.py:68
  178.9 4.1 %fusion.47 = f32[4,384,128]{2,1,0:T(8,128)} fusion(f32[4,768,384]{2,1,0:T(8,128)S(1)} %copy-done, f32[4,384]{1,0:T(4,128)S(1)} %select_maximum_fusion.2, pred[384,768]{0,1:T(8,128)(4,1)S(1)} %compare_and_fusion.2, f32[4,384,128]{2,1,0:T(8,128)} %get-tuple-element.352, bf16[3072,4,128]{0,2,1:T(8,128)(2,1)} %get-tuple-element.369, s32[]{:T(128)S(6)} %select_n.78, ...), kind=kOutput, calls=%fused_computation.8.clone.1 | convolution fusion | flops 308477952 | bytes 7385093 | tf_op jit(solution)/shard_map/while/body/eval_jaxpr/hqk,khd->hqd/dot_general | solution.py:69
  183.3 4.4 %fusion.44 = (f32[4,384]{1,0:T(4,128)S(1)}, f32[4,768,384]{2,1,0:T(8,128)}) fusion(pred[384,768]{0,1:T(8,128)(4,1)S(1)} %compare_and_fusion.2, bf16[384,4,128]{2,0,1:T(8,128)(2,1)S(1)} %get-tuple-element.368, bf16[3072,4,128]{0,2,1:T(8,128)(2,1)} %get-tuple-element.367, s32[]{:T(128)S(6)} %select_n.78), kind=kOutput, calls=%fused_computation.3.clone.1 | convolution fusion | flops 305527296 | bytes 6199300 | tf_op jit(solution)/shard_map/while/body/eval_jaxpr/qhd,khd->hqk/dot_general | solution.py:61
  187.7 3.7 %fusion.45 = f32[4,384]{1,0:T(4,128)S(1)} fusion(f32[4,768,384]{2,1,0:T(8,128)} %get-tuple-element.333, f32[4,384]{1,0:T(4,128)S(1)} %select_maximum_fusion.2, pred[384,768]{0,1:T(8,128)(4,1)S(1)} %compare_and_fusion.2), kind=kLoop, calls=%fused_computation.5.clone.1 | loop fusion | flops 5896704 | bytes 5025792 | tf_op jit(solution)/shard_map/while/body/eval_jaxpr/reduce_sum | solution.py:68
  191.5 4.1 %fusion.47 = f32[4,384,128]{2,1,0:T(8,128)} fusion(f32[4,768,384]{2,1,0:T(8,128)S(1)} %copy-done, f32[4,384]{1,0:T(4,128)S(1)} %select_maximum_fusion.2, pred[384,768]{0,1:T(8,128)(4,1)S(1)} %compare_and_fusion.2, f32[4,384,128]{2,1,0:T(8,128)} %get-tuple-element.352, bf16[3072,4,128]{0,2,1:T(8,128)(2,1)} %get-tuple-element.369, s32[]{:T(128)S(6)} %select_n.78, ...), kind=kOutput, calls=%fused_computation.8.clone.1 | convolution fusion | flops 308477952 | bytes 7385093 | tf_op jit(solution)/shard_map/while/body/eval_jaxpr/hqk,khd->hqd/dot_general | solution.py:69
  195.5 1.4 copy.36
  197.0 0.8 divide_convert_fusion
  197.8 1.0 copy.37
  198.9 1.0 copy.38
  199.8 35.2 %all-gather.11.cloned.1.call-done = bf16[384,2048]{0,1:T(8,128)(2,1)} async-done(((bf16[384,512]{0,1:T(8,128)(2,1)}), bf16[384,2048]{0,1:T(8,128)(2,1)}) %all-gather.11.cloned.1.call-update) | async-done | bytes 1572880 | tf_op jit(solution)/shard_map/all_gather | solution.py:97
  235.0 3.8 %convolution_convert_fusion = bf16[384,512]{1,0:T(8,128)(2,1)} fusion(bf16[384,2048]{0,1:T(8,128)(2,1)} %all-gather.11.cloned.1.call-done, bf16[2048,512]{1,0:T(8,128)(2,1)} %all-gather.13.cloned.1.call-done), kind=kOutput, calls=%fused_computation.36 | convolution fusion | flops 805502976 | bytes 4063232 | tf_op jit(solution)/shard_map/dot_general | solution.py:99
  (80 shorter events, 7.2 us)
Async XLA Ops:
  7.2 38.6 %copy-start.2 = (bf16[384,512]{1,0:T(8,128)(2,1)S(1)}, bf16[384,512]{1,0:T(8,128)(2,1)}, u32[]{:S(2)}) copy-start(bf16[384,512]{1,0:T(8,128)(2,1)} %param.7) | copy-start | bytes 1179652
  7.2 51.0 %all-gather.7.cloned.1.call-start = ((), (), s32[]{:S(2)}) async-start(), calls=%async_computation | async-start | bytes 7077888 | tf_op jit(solution)/shard_map/all_gather | solution.py:41
  7.9 102.0 %all-gather.9.cloned.1.call-start = ((), (), s32[]{:S(2)}) async-start(), calls=%async_computation.1 | async-start | bytes 3538944 | tf_op jit(solution)/shard_map/all_gather | solution.py:83
  8.0 14.4 %collective-permute-start = (bf16[384,512]{1,0:T(8,128)(2,1)}, bf16[384,512]{1,0:T(8,128)(2,1)S(1)}, u32[]{:S(2)}, u32[]{:S(2)}) collective-permute-start(bf16[384,512]{1,0:T(8,128)(2,1)} %param.7), channel_id=1, source_target_pairs={{0,1},{1,2},{2,3},{3,0},{4,5},{5,6},{6,7},{7,4},{8,9},{9,10},{10,1... | collective-permute-start | bytes 1179656 | tf_op jit(solution)/shard_map/ppermute | solution.py:34
  22.4 12.1 %collective-permute-start.1 = (bf16[384,512]{1,0:T(8,128)(2,1)S(1)}, bf16[384,512]{1,0:T(8,128)(2,1)S(1)}, u32[]{:S(2)}, u32[]{:S(2)}) collective-permute-start(bf16[384,512]{1,0:T(8,128)(2,1)S(1)} %collective-permute-done), channel_id=1, source_target_pairs={{0,1},{1,2},{2,3},{3,0},{4,5},{5,6},{6,7},{7,4},{8,9},{9,10},{10,1... | collective-permute-start | bytes 1179656 | tf_op jit(solution)/shard_map/ppermute | solution.py:34
  34.5 11.2 %collective-permute-start.2 = (bf16[384,512]{1,0:T(8,128)(2,1)S(1)}, bf16[384,512]{1,0:T(8,128)(2,1)S(1)}, u32[]{:S(2)}, u32[]{:S(2)}) collective-permute-start(bf16[384,512]{1,0:T(8,128)(2,1)S(1)} %collective-permute-done.1), channel_id=1, source_target_pairs={{0,1},{1,2},{2,3},{3,0},{4,5},{5,6},{6,7},{7,4},{8,9},{9,10},{10,1... | collective-permute-start | bytes 1179656 | tf_op jit(solution)/shard_map/ppermute | solution.py:34
  46.0 1.6 copy-start.3
  48.1 20.7 %copy-start.6 = (f32[2048]{0:T(1024)S(1)}, f32[2048]{0:T(1024)}, u32[]{:S(2)}) copy-start(f32[2048]{0:T(1024)} %param.8) | copy-start | bytes 24580
  75.0 0.9 copy-start.4
  75.0 0.9 copy-start.5
  76.9 68.3 %all-gather.15.cloned.1.call-start = ((), (), s32[]{:S(2)}) async-start(), calls=%async_computation.4 | async-start | bytes 3538944 | tf_op jit(solution)/shard_map/all_gather | solution.py:84
  77.8 122.0 %all-gather.13.cloned.1.call-start = ((), (), s32[]{:S(2)}) async-start(), calls=%async_computation.3 | async-start | bytes 2359296 | tf_op jit(solution)/shard_map/all_gather | solution.py:100
  78.4 156.7 %all-gather.11.cloned.1.call-start = ((), (), s32[]{:S(2)}) async-start(), calls=%async_computation.2 | async-start | bytes 1966080 | tf_op jit(solution)/shard_map/all_gather | solution.py:97
  149.9 3.8 %copy-start = (f32[4,768,384]{2,1,0:T(8,128)S(1)}, f32[4,768,384]{2,1,0:T(8,128)}, u32[]{:S(2)}) copy-start(f32[4,768,384]{2,1,0:T(8,128)} %get-tuple-element.333) | copy-start | bytes 14155780 | tf_op jit(solution)/shard_map/while
  162.3 4.1 %copy-start = (f32[4,768,384]{2,1,0:T(8,128)S(1)}, f32[4,768,384]{2,1,0:T(8,128)}, u32[]{:S(2)}) copy-start(f32[4,768,384]{2,1,0:T(8,128)} %get-tuple-element.333) | copy-start | bytes 14155780 | tf_op jit(solution)/shard_map/while
  175.2 3.8 %copy-start = (f32[4,768,384]{2,1,0:T(8,128)S(1)}, f32[4,768,384]{2,1,0:T(8,128)}, u32[]{:S(2)}) copy-start(f32[4,768,384]{2,1,0:T(8,128)} %get-tuple-element.333) | copy-start | bytes 14155780 | tf_op jit(solution)/shard_map/while
  187.7 3.8 %copy-start = (f32[4,768,384]{2,1,0:T(8,128)S(1)}, f32[4,768,384]{2,1,0:T(8,128)}, u32[]{:S(2)}) copy-start(f32[4,768,384]{2,1,0:T(8,128)} %get-tuple-element.333) | copy-start | bytes 14155780 | tf_op jit(solution)/shard_map/while
  195.5 2.3 copy-start.1
Sparse Core Ops, SparseCore 0:
  9.9 48.2 all-gather.6
  77.0 32.8 all-gather.8
  112.3 32.8 all-gather.14
  146.9 27.8 all-gather.12
  198.0 37.0 all-gather.10
